TPU v7x, 32 devices: a whole 2x2x4 slice. The times are simulated.
32 devices in a mesh: row: 2 (over y), col: 8 (over z, x), depth: 2 (over core).
Axes of the slice: x: 2, y: 2, z: 4, core: 2. Of those that a mesh axis runs over, the one named last changes fastest.
Arguments:
- a_tiles: bfloat16 [2, 16, 8, 2, 128, 128], P('row', ('col', 'depth')), may hold values from -1.5 to 1.5
- a_cols: int32 [2, 16, 8, 2], P('row', ('col', 'depth')), may hold values from 0 to 15, as said below
- a_count: int32 [2, 16, 8], P('row', ('col', 'depth')), may hold values from 0 to 2, as said below
- b_tiles: bfloat16 [4, 2, 2, 8, 16, 1, 128, 128], P(None, 'row', 'depth', 'col'), may hold values from -1.5 to 1.5
- b_cols: int32 [4, 2, 2, 8, 16, 1], P(None, 'row', 'depth', 'col'), may hold values from 0 to 11, as said below
- b_count: int32 [4, 2, 2, 8, 16], P(None, 'row', 'depth', 'col'), may hold values from 0 to 1, as said below
Outputs:
- product: bfloat16 [2048, 12288], P(('row', 'depth'), 'col')
Inputs may be any that keep to these rules, and one draw needn't show every extreme that they name: The entries of a_cols for one row group, inner panel and block row are distinct. `a_count`: some block row holds 2 blocks in every draw. The entries of b_cols for one inner block row are distinct. `b_count`: some inner block row holds 1 block in every draw.
All inputs are finite; a program needn't handle non-finite values.
Results may differ from a plain program's by a relative error of at most 0.001.
Values may be sent and summed in bfloat16 or wider, within the bound.
A program may use at most 128 MiB of HBM per device.

v0:
```python
import math

import jax
import jax.numpy as jnp
from jax import lax
from jax.sharding import PartitionSpec as P

BC = 12
SHIFTS = 4


def for_sending(array):
    return jax.tree.map(lambda a: a.astype(jnp.bfloat16) if a.dtype == jnp.float32 else a, array)


def shifted(value, axis, steps):
    count = lax.axis_size(axis)
    pairs = [(source, (source + steps) % count) for source in range(count)]
    return lax.ppermute(value, axis, pairs)


def dense_panel(tiles_b, cols_b, count_b, width):
    slot_ids = lax.broadcasted_iota(jnp.int32, cols_b.shape, 1)
    valid_slot = slot_ids < count_b[:, None]
    targets = lax.broadcasted_iota(jnp.int32, (1, 1, width), 2)
    placing = jnp.logical_and(cols_b[:, :, None] == targets, valid_slot[:, :, None]).astype(
        jnp.bfloat16
    )
    spread = jnp.einsum("kuc,kuab->kacb", placing, tiles_b, preferred_element_type=jnp.float32)
    inner_blocks = tiles_b.shape[0]
    tile_size = tiles_b.shape[2]
    return spread.astype(jnp.bfloat16).reshape(inner_blocks, tile_size, width * tile_size)


def panel_product(tiles_a, cols_a, count_a, rows_dense):
    block_rows = tiles_a.shape[0]
    per_row = tiles_a.shape[1]
    tile_size = tiles_a.shape[2]
    slot_ids = lax.broadcasted_iota(jnp.int32, cols_a.shape, 1)
    valid_slot = slot_ids < count_a[:, None]
    masked = jnp.where(valid_slot[:, :, None, None], tiles_a, jnp.zeros_like(tiles_a))
    group_rows = math.gcd(block_rows, 4)

    def one_group(pieces):
        tiles_part, cols_part = pieces
        chosen = jnp.take(rows_dense, cols_part, axis=0)
        return jnp.einsum("rtab,rtbn->ran", tiles_part, chosen, preferred_element_type=jnp.float32)

    grouped = lax.map(
        one_group,
        (
            masked.reshape(block_rows // group_rows, group_rows, per_row, tile_size, tile_size),
            cols_a.reshape(block_rows // group_rows, group_rows, per_row),
        ),
    )
    return grouped.reshape(block_rows, tile_size, rows_dense.shape[2])


def roll_slots(stack, offset):
    slot_total = stack[0].shape[0]
    return tuple(
        (
            lax.dynamic_slice_in_dim(
                jnp.concatenate([member, member], 0), offset % slot_total, slot_total, 0
            )
            for member in stack
        )
    )


def select_if(flag, fresh, stale):
    return tuple((jnp.where(flag, new_part, old_part) for new_part, old_part in zip(fresh, stale)))


def local(a_tiles, a_cols, a_count, b_tiles, b_cols, b_count):
    rows_axis = lax.axis_size("row")
    cols_axis = lax.axis_size("col")
    row_group = lax.axis_index("row")
    col_group = lax.axis_index("col")
    tiles_a = a_tiles[0, 0]
    cols_a = a_cols[0, 0]
    count_a = a_count[0, 0]
    tiles_b = b_tiles[:, 0, 0, 0]
    cols_b = b_cols[:, 0, 0, 0]
    count_b = b_count[:, 0, 0, 0]
    for bit_pos in range((rows_axis - 1).bit_length()):
        stride = 1 << bit_pos
        moved = (
            shifted(tiles_a, "col", cols_axis - stride),
            shifted(for_sending(cols_a), "col", cols_axis - stride).astype(cols_a.dtype),
            shifted(for_sending(count_a), "col", cols_axis - stride).astype(count_a.dtype),
        )
        tiles_a, cols_a, count_a = select_if(
            row_group // stride % 2 == 1, moved, (tiles_a, cols_a, count_a)
        )
    for bit_pos in range((cols_axis - 1).bit_length()):
        stride = 1 << bit_pos
        nearby = stride % rows_axis
        if nearby:
            moved = (
                shifted(tiles_b, "row", rows_axis - nearby),
                shifted(for_sending(cols_b), "row", rows_axis - nearby).astype(cols_b.dtype),
                shifted(for_sending(count_b), "row", rows_axis - nearby).astype(count_b.dtype),
            )
        else:
            moved = (tiles_b, cols_b, count_b)
        moved = roll_slots(moved, (row_group + stride) // rows_axis)
        tiles_b, cols_b, count_b = select_if(
            col_group // stride % 2 == 1, moved, (tiles_b, cols_b, count_b)
        )
    tile_size = tiles_a.shape[2]
    running = jnp.zeros((tiles_a.shape[0], tile_size, BC * tile_size), jnp.float32)
    for turn_no in range(SHIFTS):
        current_tiles = tiles_b[0]
        current_cols = cols_b[0]
        current_count = count_b[0]
        rows_dense = dense_panel(current_tiles, current_cols, current_count, BC)
        running = running + panel_product(tiles_a, cols_a, count_a, rows_dense)
        if turn_no + 1 < SHIFTS:
            tiles_a, cols_a, count_a = (
                shifted(tiles_a, "col", cols_axis - 1),
                shifted(for_sending(cols_a), "col", cols_axis - 1).astype(cols_a.dtype),
                shifted(for_sending(count_a), "col", cols_axis - 1).astype(count_a.dtype),
            )
            moved = (
                shifted(tiles_b, "row", rows_axis - 1),
                shifted(for_sending(cols_b), "row", rows_axis - 1).astype(cols_b.dtype),
                shifted(for_sending(count_b), "row", rows_axis - 1).astype(count_b.dtype),
            )
            tiles_b, cols_b, count_b = roll_slots(moved, (row_group + 1) // rows_axis)
    flat_running = running.reshape(-1, running.shape[2])
    summed = lax.psum(flat_running, "depth")
    half_rows = flat_running.shape[0] // lax.axis_size("depth")
    own_rows = lax.dynamic_slice_in_dim(summed, lax.axis_index("depth") * half_rows, half_rows, 0)
    return own_rows.astype(jnp.bfloat16)


def solution(mesh):
    placed = (
        P("row", ("col", "depth"), None, None, None, None),
        P("row", ("col", "depth"), None, None),
        P("row", ("col", "depth"), None),
        P(None, "row", "depth", "col", None, None, None, None),
        P(None, "row", "depth", "col", None, None),
        P(None, "row", "depth", "col", None),
    )
    return jax.shard_map(
        local, mesh=mesh, in_specs=placed, out_specs=P(("row", "depth"), "col"), check_vma=False
    )
```

profile of v0, /device:TPU:2, one launch (start us, length us, event | category | flops | bytes accessed | tf_op | source)
XLA Modules:
  0.0 306.9 jit_solution(8262394096898452640)
XLA Ops:
  0.1 5.1 %collective-permute-start.2 = (s32[8,2]{0,1:T(2,128)}, s32[8,2]{0,1:T(2,128)S(1)}, u32[]{:S(2)}, u32[]{:S(2)}) collective-permute-start(s32[8,2]{0,1:T(2,128)} %bitcast.189), channel_id=1, source_target_pairs={{0,14},{2,0},{4,2},{6,4},{8,6},{10,8},{12,10},{14,12},{1,15},{3,1}... | collective-permute-start | bytes 200 | tf_op jit(solution)/shard_map/ppermute | solution.py:19
  7.7 3.0 copy.31
  10.8 1.6 collective-permute-start.3
  13.9 7.0 %collective-permute-done.6 = s32[8]{0:T(128)S(1)} collective-permute-done((s32[8]{0:T(128)S(1)}, s32[8]{0:T(128)S(1)}, u32[]{:S(2)}, u32[]{:S(2)}) %collective-permute-start.6) | collective-permute-done | bytes 64 | tf_op jit(solution)/shard_map/ppermute | solution.py:19
  21.0 4.5 %collective-permute-done.12 = s32[8]{0:T(128)S(1)} collective-permute-done((s32[8]{0:T(128)S(1)}, s32[8]{0:T(128)S(1)}, u32[]{:S(2)}, u32[]{:S(2)}) %collective-permute-start.12) | collective-permute-done | bytes 64 | tf_op jit(solution)/shard_map/ppermute | solution.py:19
  26.1 3.9 %collective-permute-done.18 = s32[8]{0:T(128)S(1)} collective-permute-done((s32[8]{0:T(128)S(1)}, s32[8]{0:T(128)S(1)}, u32[]{:S(2)}, u32[]{:S(2)}) %collective-permute-start.18) | collective-permute-done | bytes 64 | tf_op jit(solution)/shard_map/ppermute | solution.py:19
  30.0 2.3 collective-permute-start.8
  32.4 2.1 collective-permute-done.8
  34.5 4.1 %collective-permute-start.14 = (s32[8,2]{0,1:T(2,128)S(1)}, s32[8,2]{0,1:T(2,128)S(1)}, u32[]{:S(2)}, u32[]{:S(2)}) collective-permute-start(s32[8,2]{0,1:T(2,128)S(1)} %collective-permute-done.8), channel_id=1, source_target_pairs={{0,14},{2,0},{4,2},{6,4},{8,6},{10,8},{12,10},{14,12},{1,15},{3,1}... | collective-permute-start | bytes 200 | tf_op jit(solution)/shard_map/ppermute | solution.py:19
  40.0 5.0 %collective-permute-start.20 = (s32[8,2]{0,1:T(2,128)S(1)}, s32[8,2]{0,1:T(2,128)S(1)}, u32[]{:S(2)}, u32[]{:S(2)}) collective-permute-start(s32[8,2]{0,1:T(2,128)S(1)} %collective-permute-done.14), channel_id=1, source_target_pairs={{0,14},{2,0},{4,2},{6,4},{8,6},{10,8},{12,10},{14,12},{1,15},{3,1}... | collective-permute-start | bytes 200 | tf_op jit(solution)/shard_map/ppermute | solution.py:19
  47.5 9.4 %collective-permute-done.10 = s32[4,16,1]{1,0,2:T(4,128)S(1)} collective-permute-done((s32[4,16,1]{1,0,2:T(4,128)S(1)}, s32[4,16,1]{1,0,2:T(4,128)S(1)}, u32[]{:S(2)}, u32[]{:S(2)}) %collective-permute-start.10) | collective-permute-done | bytes 288 | tf_op jit(solution)/shard_map/ppermute | solution.py:19
  66.7 11.0 %collective-permute-done.7 = bf16[8,2,128,128]{3,2,1,0:T(8,128)(2,1)S(1)} collective-permute-done((bf16[8,2,128,128]{3,2,1,0:T(8,128)(2,1)S(1)}, bf16[8,2,128,128]{3,2,1,0:T(8,128)(2,1)S(1)}, u32[]{:S(2)}, u32[]{:S(2)}) %collective-permute-start.7) | collective-permute-done | bytes 524320 | tf_op jit(solution)/shard_map/ppermute | solution.py:19
  80.1 11.2 %collective-permute-done.13 = bf16[8,2,128,128]{3,2,1,0:T(8,128)(2,1)S(1)} collective-permute-done((bf16[8,2,128,128]{3,2,1,0:T(8,128)(2,1)S(1)}, bf16[8,2,128,128]{3,2,1,0:T(8,128)(2,1)S(1)}, u32[]{:S(2)}, u32[]{:S(2)}) %collective-permute-start.13) | collective-permute-done | bytes 524320 | tf_op jit(solution)/shard_map/ppermute | solution.py:19
  93.6 2.4 fusion.47
  96.9 2.2 fusion.43
  100.5 2.2 fusion.51
  103.6 3.4 %broadcast.166.clone.2 = f32[2,4,128,1536]{3,2,1,0:T(8,128)} broadcast(f32[]{:T(128)} %constant.191.clone.1), dimensions={} | broadcast | bytes 6291460 | tf_op jit(solution)/shard_map/broadcast.11
  107.0 34.5 %while.44 = (s32[]{:T(128)}, f32[2,4,128,1536]{3,2,1,0:T(8,128)}, bf16[2,4,2,128,128]{4,3,2,1,0:T(8,128)(2,1)}, s32[2,4,2]{1,0,2:T(2,128)S(1)}, f32[16,12]{1,0:T(8,128)S(1)}, /*index=5*/f32[16,128,128]{1,2,0:T(8,128)}, s32[]{:T(128)}) while((s32[]{:T(128)}, f32[2,4,128,1536]{3,2,1,0:T(8,128)}, ...), condition=%wide.region_1.3_spmd.clone, body=%wide.region_0.2_spmd.clone.sunk | while | flops 410518592 | bytes 26482904 | solution.py:49
  107.3 5.0 %multiply_convert_fusion.8 = bf16[16,128,128,12]{1,2,3,0:T(8,128)(2,1)} fusion(f32[16,12]{1,0:T(8,128)S(1)} %get-tuple-element.488, f32[16,128,128]{1,2,0:T(8,128)} %get-tuple-element.489), kind=kLoop, calls=%fused_computation.8.clone.1 | loop fusion | flops 6291456 | bytes 7340800 | tf_op jit(solution)/shard_map/convert_element_type | solution.py:32
  112.3 5.4 %gather_fusion = bf16[8,128,1536]{1,2,0:T(8,128)(2,1)} fusion(bf16[16,128,1536]{1,2,0:T(8,128)(2,1)} %bitcast.162, s32[1024]{0:T(1024)S(1)} %pad_clamp_fusion.8), kind=kCustom, calls=%fused_computation.clone.clone.1 | custom fusion | bytes 6291488 | tf_op jit(solution)/shard_map/while/body/eval_jaxpr/jit(_take)/gather | solution.py:46
  117.7 3.2 %copy.57 = bf16[4,2,128,1536]{3,2,1,0:T(8,128)(2,1)S(1)} copy(bf16[4,2,128,1536]{2,3,1,0:T(8,128)(2,1)} %bitcast.166) | data formatting | bytes 6291456 | tf_op jit(solution)/shard_map/while/body/eval_jaxpr/jit(_take)/gather | solution.py:46
  120.9 3.4 %fusion.80 = f32[2,4,128,1536]{3,2,1,0:T(8,128)} fusion(f32[2,4,128,1536]{3,2,1,0:T(8,128)} %get-tuple-element.478, s32[]{:T(128)S(6)} %copy.86, bf16[4,2,128,1536]{3,2,1,0:T(8,128)(2,1)S(1)} %copy.57, pred[4,2]{1,0:T(4,128)(4,1)S(1)} %copy.58, bf16[2,4,2,128,128]{4,3,2,1,0:T(8,128)(2,1)} %get-tuple-element.486), kind=kOutput, calls=%fused_computation.10.clone.1 | convolution fusion | flops 404226048 | bytes 6554632 | tf_op jit(solution)/shard_map/while/body/eval_jaxpr/rtab,rtbn->ran/dot_general | solution.py:47
  124.6 5.0 %multiply_convert_fusion.8 = bf16[16,128,128,12]{1,2,3,0:T(8,128)(2,1)} fusion(f32[16,12]{1,0:T(8,128)S(1)} %get-tuple-element.488, f32[16,128,128]{1,2,0:T(8,128)} %get-tuple-element.489), kind=kLoop, calls=%fused_computation.8.clone.1 | loop fusion | flops 6291456 | bytes 7340800 | tf_op jit(solution)/shard_map/convert_element_type | solution.py:32
  129.6 5.4 %gather_fusion = bf16[8,128,1536]{1,2,0:T(8,128)(2,1)} fusion(bf16[16,128,1536]{1,2,0:T(8,128)(2,1)} %bitcast.162, s32[1024]{0:T(1024)S(1)} %pad_clamp_fusion.8), kind=kCustom, calls=%fused_computation.clone.clone.1 | custom fusion | bytes 6291488 | tf_op jit(solution)/shard_map/while/body/eval_jaxpr/jit(_take)/gather | solution.py:46
  135.0 3.2 %copy.57 = bf16[4,2,128,1536]{3,2,1,0:T(8,128)(2,1)S(1)} copy(bf16[4,2,128,1536]{2,3,1,0:T(8,128)(2,1)} %bitcast.166) | data formatting | bytes 6291456 | tf_op jit(solution)/shard_map/while/body/eval_jaxpr/jit(_take)/gather | solution.py:46
  138.2 3.4 %fusion.80 = f32[2,4,128,1536]{3,2,1,0:T(8,128)} fusion(f32[2,4,128,1536]{3,2,1,0:T(8,128)} %get-tuple-element.478, s32[]{:T(128)S(6)} %copy.86, bf16[4,2,128,1536]{3,2,1,0:T(8,128)(2,1)S(1)} %copy.57, pred[4,2]{1,0:T(4,128)(4,1)S(1)} %copy.58, bf16[2,4,2,128,128]{4,3,2,1,0:T(8,128)(2,1)} %get-tuple-element.486), kind=kOutput, calls=%fused_computation.10.clone.1 | convolution fusion | flops 404226048 | bytes 6554632 | tf_op jit(solution)/shard_map/while/body/eval_jaxpr/rtab,rtbn->ran/dot_general | solution.py:47
  141.6 3.7 %fusion.41 = bf16[4,16,1,128,128]{3,4,1,2,0:T(8,128)(2,1)} fusion(s32[]{:T(128)S(6)} %select_n.231, bf16[4,16,1,128,128]{3,4,1,2,0:T(8,128)(2,1)} %collective-permute-done.9), kind=kLoop, calls=%fused_computation.79 | loop fusion | flops 1048576 | bytes 4194308 | tf_op jit(solution)/shard_map/concatenate | solution.py:64
  145.3 2.1 fusion.50
  147.9 3.5 %broadcast.166.clone.3 = f32[2,4,128,1536]{3,2,1,0:T(8,128)} broadcast(f32[]{:T(128)} %constant.191.clone.1), dimensions={} | broadcast | bytes 6291460 | tf_op jit(solution)/shard_map/broadcast.11
  151.4 34.5 %while.45 = (s32[]{:T(128)}, f32[2,4,128,1536]{3,2,1,0:T(8,128)}, bf16[2,4,2,128,128]{4,3,2,1,0:T(8,128)(2,1)}, s32[2,4,2]{1,0,2:T(2,128)S(1)}, f32[16,12]{1,0:T(8,128)S(1)}, /*index=5*/f32[16,128,128]{1,2,0:T(8,128)}, s32[]{:T(128)}) while((s32[]{:T(128)}, f32[2,4,128,1536]{3,2,1,0:T(8,128)}, ...), condition=%wide.region_3.5_spmd.clone, body=%wide.region_2.4_spmd.clone.sunk | while | flops 410518592 | bytes 26482904 | solution.py:49
  151.7 4.9 %multiply_convert_fusion.9 = bf16[16,128,128,12]{1,2,3,0:T(8,128)(2,1)} fusion(f32[16,12]{1,0:T(8,128)S(1)} %get-tuple-element.509, f32[16,128,128]{1,2,0:T(8,128)} %get-tuple-element.510), kind=kLoop, calls=%fused_computation.22.clone.1 | loop fusion | flops 6291456 | bytes 7340800 | tf_op jit(solution)/shard_map/convert_element_type | solution.py:32
  156.7 5.4 %gather_fusion.1 = bf16[8,128,1536]{1,2,0:T(8,128)(2,1)} fusion(bf16[16,128,1536]{1,2,0:T(8,128)(2,1)} %bitcast.163, s32[1024]{0:T(1024)S(1)} %pad_clamp_fusion.9), kind=kCustom, calls=%fused_computation.1.clone.clone.1 | custom fusion | bytes 6291488 | tf_op jit(solution)/shard_map/while/body/eval_jaxpr/jit(_take)/gather | solution.py:46
  162.1 3.2 %copy.60 = bf16[4,2,128,1536]{3,2,1,0:T(8,128)(2,1)S(1)} copy(bf16[4,2,128,1536]{2,3,1,0:T(8,128)(2,1)} %bitcast.167) | data formatting | bytes 6291456 | tf_op jit(solution)/shard_map/while/body/eval_jaxpr/jit(_take)/gather | solution.py:46
  165.3 3.3 %fusion.83 = f32[2,4,128,1536]{3,2,1,0:T(8,128)} fusion(f32[2,4,128,1536]{3,2,1,0:T(8,128)} %get-tuple-element.499, s32[]{:T(128)S(6)} %copy.92, bf16[4,2,128,1536]{3,2,1,0:T(8,128)(2,1)S(1)} %copy.60, pred[4,2]{1,0:T(4,128)(4,1)S(1)} %copy.61, bf16[2,4,2,128,128]{4,3,2,1,0:T(8,128)(2,1)} %get-tuple-element.507), kind=kOutput, calls=%fused_computation.24.clone.1 | convolution fusion | flops 404226048 | bytes 6554632 | tf_op jit(solution)/shard_map/while/body/eval_jaxpr/rtab,rtbn->ran/dot_general | solution.py:47
  168.9 4.9 %multiply_convert_fusion.9 = bf16[16,128,128,12]{1,2,3,0:T(8,128)(2,1)} fusion(f32[16,12]{1,0:T(8,128)S(1)} %get-tuple-element.509, f32[16,128,128]{1,2,0:T(8,128)} %get-tuple-element.510), kind=kLoop, calls=%fused_computation.22.clone.1 | loop fusion | flops 6291456 | bytes 7340800 | tf_op jit(solution)/shard_map/convert_element_type | solution.py:32
  173.9 5.4 %gather_fusion.1 = bf16[8,128,1536]{1,2,0:T(8,128)(2,1)} fusion(bf16[16,128,1536]{1,2,0:T(8,128)(2,1)} %bitcast.163, s32[1024]{0:T(1024)S(1)} %pad_clamp_fusion.9), kind=kCustom, calls=%fused_computation.1.clone.clone.1 | custom fusion | bytes 6291488 | tf_op jit(solution)/shard_map/while/body/eval_jaxpr/jit(_take)/gather | solution.py:46
  179.3 3.2 %copy.60 = bf16[4,2,128,1536]{3,2,1,0:T(8,128)(2,1)S(1)} copy(bf16[4,2,128,1536]{2,3,1,0:T(8,128)(2,1)} %bitcast.167) | data formatting | bytes 6291456 | tf_op jit(solution)/shard_map/while/body/eval_jaxpr/jit(_take)/gather | solution.py:46
  182.5 3.4 %fusion.83 = f32[2,4,128,1536]{3,2,1,0:T(8,128)} fusion(f32[2,4,128,1536]{3,2,1,0:T(8,128)} %get-tuple-element.499, s32[]{:T(128)S(6)} %copy.92, bf16[4,2,128,1536]{3,2,1,0:T(8,128)(2,1)S(1)} %copy.60, pred[4,2]{1,0:T(4,128)(4,1)S(1)} %copy.61, bf16[2,4,2,128,128]{4,3,2,1,0:T(8,128)(2,1)} %get-tuple-element.507), kind=kOutput, calls=%fused_computation.24.clone.1 | convolution fusion | flops 404226048 | bytes 6554632 | tf_op jit(solution)/shard_map/while/body/eval_jaxpr/rtab,rtbn->ran/dot_general | solution.py:47
  185.9 3.7 %fusion.40 = bf16[4,16,1,128,128]{3,4,1,2,0:T(8,128)(2,1)} fusion(s32[]{:T(128)S(6)} %select_n.231, bf16[4,16,1,128,128]{3,4,1,2,0:T(8,128)(2,1)} %collective-permute-done.15), kind=kLoop, calls=%fused_computation.78 | loop fusion | flops 1048576 | bytes 4194308 | tf_op jit(solution)/shard_map/concatenate | solution.py:64
  189.5 2.1 fusion.49
  191.7 2.1 collective-permute-start.21
  193.7 3.4 %broadcast.166.clone.1 = f32[2,4,128,1536]{3,2,1,0:T(8,128)} broadcast(f32[]{:T(128)} %constant.191.clone.1), dimensions={} | broadcast | bytes 6291460 | tf_op jit(solution)/shard_map/broadcast.11
  197.1 34.5 %while.46 = (s32[]{:T(128)}, f32[2,4,128,1536]{3,2,1,0:T(8,128)}, bf16[2,4,2,128,128]{4,3,2,1,0:T(8,128)(2,1)}, s32[2,4,2]{1,0,2:T(2,128)S(1)}, f32[16,12]{1,0:T(8,128)S(1)}, /*index=5*/f32[16,128,128]{1,2,0:T(8,128)}, s32[]{:T(128)}) while((s32[]{:T(128)}, f32[2,4,128,1536]{3,2,1,0:T(8,128)}, ...), condition=%wide.region_5.7_spmd.clone, body=%wide.region_4.6_spmd.clone.sunk | while | flops 410518592 | bytes 26482904 | solution.py:49
  197.4 5.0 %multiply_convert_fusion.10 = bf16[16,128,128,12]{1,2,3,0:T(8,128)(2,1)} fusion(f32[16,12]{1,0:T(8,128)S(1)} %get-tuple-element.467, f32[16,128,128]{1,2,0:T(8,128)} %get-tuple-element.468), kind=kLoop, calls=%fused_computation.36.clone.1 | loop fusion | flops 6291456 | bytes 7340800 | tf_op jit(solution)/shard_map/convert_element_type | solution.py:32
  202.4 5.4 %gather_fusion.2 = bf16[8,128,1536]{1,2,0:T(8,128)(2,1)} fusion(bf16[16,128,1536]{1,2,0:T(8,128)(2,1)} %bitcast.164, s32[1024]{0:T(1024)S(1)} %pad_clamp_fusion.10), kind=kCustom, calls=%fused_computation.2.clone.clone.1 | custom fusion | bytes 6291488 | tf_op jit(solution)/shard_map/while/body/eval_jaxpr/jit(_take)/gather | solution.py:46
  207.8 3.2 %copy.63 = bf16[4,2,128,1536]{3,2,1,0:T(8,128)(2,1)S(1)} copy(bf16[4,2,128,1536]{2,3,1,0:T(8,128)(2,1)} %bitcast.168) | data formatting | bytes 6291456 | tf_op jit(solution)/shard_map/while/body/eval_jaxpr/jit(_take)/gather | solution.py:46
  211.0 3.3 %fusion.86 = f32[2,4,128,1536]{3,2,1,0:T(8,128)} fusion(f32[2,4,128,1536]{3,2,1,0:T(8,128)} %get-tuple-element.457, s32[]{:T(128)S(6)} %copy.80, bf16[4,2,128,1536]{3,2,1,0:T(8,128)(2,1)S(1)} %copy.63, pred[4,2]{1,0:T(4,128)(4,1)S(1)} %copy.64, bf16[2,4,2,128,128]{4,3,2,1,0:T(8,128)(2,1)} %get-tuple-element.465), kind=kOutput, calls=%fused_computation.38.clone.1 | convolution fusion | flops 404226048 | bytes 6554632 | tf_op jit(solution)/shard_map/while/body/eval_jaxpr/rtab,rtbn->ran/dot_general | solution.py:47
  214.7 5.0 %multiply_convert_fusion.10 = bf16[16,128,128,12]{1,2,3,0:T(8,128)(2,1)} fusion(f32[16,12]{1,0:T(8,128)S(1)} %get-tuple-element.467, f32[16,128,128]{1,2,0:T(8,128)} %get-tuple-element.468), kind=kLoop, calls=%fused_computation.36.clone.1 | loop fusion | flops 6291456 | bytes 7340800 | tf_op jit(solution)/shard_map/convert_element_type | solution.py:32
  219.6 5.4 %gather_fusion.2 = bf16[8,128,1536]{1,2,0:T(8,128)(2,1)} fusion(bf16[16,128,1536]{1,2,0:T(8,128)(2,1)} %bitcast.164, s32[1024]{0:T(1024)S(1)} %pad_clamp_fusion.10), kind=kCustom, calls=%fused_computation.2.clone.clone.1 | custom fusion | bytes 6291488 | tf_op jit(solution)/shard_map/while/body/eval_jaxpr/jit(_take)/gather | solution.py:46
  225.0 3.2 %copy.63 = bf16[4,2,128,1536]{3,2,1,0:T(8,128)(2,1)S(1)} copy(bf16[4,2,128,1536]{2,3,1,0:T(8,128)(2,1)} %bitcast.168) | data formatting | bytes 6291456 | tf_op jit(solution)/shard_map/while/body/eval_jaxpr/jit(_take)/gather | solution.py:46
  228.2 3.3 %fusion.86 = f32[2,4,128,1536]{3,2,1,0:T(8,128)} fusion(f32[2,4,128,1536]{3,2,1,0:T(8,128)} %get-tuple-element.457, s32[]{:T(128)S(6)} %copy.80, bf16[4,2,128,1536]{3,2,1,0:T(8,128)(2,1)S(1)} %copy.63, pred[4,2]{1,0:T(4,128)(4,1)S(1)} %copy.64, bf16[2,4,2,128,128]{4,3,2,1,0:T(8,128)(2,1)} %get-tuple-element.465), kind=kOutput, calls=%fused_computation.38.clone.1 | convolution fusion | flops 404226048 | bytes 6554632 | tf_op jit(solution)/shard_map/while/body/eval_jaxpr/rtab,rtbn->ran/dot_general | solution.py:47
  231.6 2.2 bitcast_convert_fusion
  233.8 3.4 %broadcast.166.clone = f32[2,4,128,1536]{3,2,1,0:T(8,128)} broadcast(f32[]{:T(128)} %constant.191.clone.1), dimensions={} | broadcast | bytes 6291460 | tf_op jit(solution)/shard_map/broadcast.11
  237.2 34.3 %while.47 = (s32[]{:T(128)}, f32[2,4,128,1536]{3,2,1,0:T(8,128)}, bf16[2,4,2,128,128]{4,3,2,1,0:T(8,128)(2,1)}, s32[2,4,2]{1,0,2:T(2,128)S(1)}, f32[16,12]{1,0:T(8,128)S(1)}, /*index=5*/f32[16,128,128]{1,2,0:T(8,128)}, s32[]{:T(128)}) while((s32[]{:T(128)}, f32[2,4,128,1536]{3,2,1,0:T(8,128)}, ...), condition=%wide.region_7.9_spmd.clone, body=%wide.region_6.8_spmd.clone.sunk | while | flops 410518592 | bytes 26482904 | solution.py:49
  237.5 4.9 %multiply_convert_fusion.11 = bf16[16,128,128,12]{1,2,3,0:T(8,128)(2,1)} fusion(f32[16,12]{1,0:T(8,128)S(1)} %get-tuple-element.446, f32[16,128,128]{1,2,0:T(8,128)} %get-tuple-element.447), kind=kLoop, calls=%fused_computation.50.clone.1 | loop fusion | flops 6291456 | bytes 7340800 | tf_op jit(solution)/shard_map/convert_element_type | solution.py:32
  242.5 5.4 %gather_fusion.3 = bf16[8,128,1536]{1,2,0:T(8,128)(2,1)} fusion(bf16[16,128,1536]{1,2,0:T(8,128)(2,1)} %bitcast.165, s32[1024]{0:T(1024)S(1)} %pad_clamp_fusion.11), kind=kCustom, calls=%fused_computation.3.clone.clone.1 | custom fusion | bytes 6291488 | tf_op jit(solution)/shard_map/while/body/eval_jaxpr/jit(_take)/gather | solution.py:46
  247.8 3.2 %copy.66 = bf16[4,2,128,1536]{3,2,1,0:T(8,128)(2,1)S(1)} copy(bf16[4,2,128,1536]{2,3,1,0:T(8,128)(2,1)} %bitcast.169) | data formatting | bytes 6291456 | tf_op jit(solution)/shard_map/while/body/eval_jaxpr/jit(_take)/gather | solution.py:46
  251.0 3.4 %fusion.89 = f32[2,4,128,1536]{3,2,1,0:T(8,128)} fusion(f32[2,4,128,1536]{3,2,1,0:T(8,128)} %get-tuple-element.436, s32[]{:T(128)S(6)} %copy.74, bf16[4,2,128,1536]{3,2,1,0:T(8,128)(2,1)S(1)} %copy.66, pred[4,2]{1,0:T(4,128)(4,1)S(1)} %copy.67, bf16[2,4,2,128,128]{4,3,2,1,0:T(8,128)(2,1)} %get-tuple-element.444), kind=kOutput, calls=%fused_computation.52.clone.1 | convolution fusion | flops 404226048 | bytes 6554632 | tf_op jit(solution)/shard_map/while/body/eval_jaxpr/rtab,rtbn->ran/dot_general | solution.py:47
  254.7 4.9 %multiply_convert_fusion.11 = bf16[16,128,128,12]{1,2,3,0:T(8,128)(2,1)} fusion(f32[16,12]{1,0:T(8,128)S(1)} %get-tuple-element.446, f32[16,128,128]{1,2,0:T(8,128)} %get-tuple-element.447), kind=kLoop, calls=%fused_computation.50.clone.1 | loop fusion | flops 6291456 | bytes 7340800 | tf_op jit(solution)/shard_map/convert_element_type | solution.py:32
  259.7 5.4 %gather_fusion.3 = bf16[8,128,1536]{1,2,0:T(8,128)(2,1)} fusion(bf16[16,128,1536]{1,2,0:T(8,128)(2,1)} %bitcast.165, s32[1024]{0:T(1024)S(1)} %pad_clamp_fusion.11), kind=kCustom, calls=%fused_computation.3.clone.clone.1 | custom fusion | bytes 6291488 | tf_op jit(solution)/shard_map/while/body/eval_jaxpr/jit(_take)/gather | solution.py:46
  265.0 3.2 %copy.66 = bf16[4,2,128,1536]{3,2,1,0:T(8,128)(2,1)S(1)} copy(bf16[4,2,128,1536]{2,3,1,0:T(8,128)(2,1)} %bitcast.169) | data formatting | bytes 6291456 | tf_op jit(solution)/shard_map/while/body/eval_jaxpr/jit(_take)/gather | solution.py:46
  268.2 3.4 %fusion.89 = f32[2,4,128,1536]{3,2,1,0:T(8,128)} fusion(f32[2,4,128,1536]{3,2,1,0:T(8,128)} %get-tuple-element.436, s32[]{:T(128)S(6)} %copy.74, bf16[4,2,128,1536]{3,2,1,0:T(8,128)(2,1)S(1)} %copy.66, pred[4,2]{1,0:T(4,128)(4,1)S(1)} %copy.67, bf16[2,4,2,128,128]{4,3,2,1,0:T(8,128)(2,1)} %get-tuple-element.444), kind=kOutput, calls=%fused_computation.52.clone.1 | convolution fusion | flops 404226048 | bytes 6554632 | tf_op jit(solution)/shard_map/while/body/eval_jaxpr/rtab,rtbn->ran/dot_general | solution.py:47
  271.5 13.8 %add_add_fusion = f32[2,4,128,1536]{3,2,1,0:T(8,128)} fusion(f32[2,4,128,1536]{3,2,1,0:T(8,128)} %get-tuple-element.117, f32[2,4,128,1536]{3,2,1,0:T(8,128)} %get-tuple-element.116, f32[2,4,128,1536]{3,2,1,0:T(8,128)} %get-tuple-element.114, f32[2,4,128,1536]{3,2,1,0:T(8,128)} %get-tuple-element.115), kind=kLoop, calls=%fused_computation.64 | loop fusion | flops 4718592 | bytes 31457280 | tf_op jit(solution)/shard_map/add | solution.py:118
  285.4 20.3 %all-reduce.1 = bf16[1024,1536]{1,0:T(8,128)(2,1)S(1)} all-reduce(f32[1024,1536]{1,0:T(8,128)} %bitcast.170), channel_id=1, replica_groups=mesh['row'=2,'col'=8,'depth'=2] {'depth'}, use_global_device_ids=true, to_apply=%region_8.10 | all-reduce | flops 1572864 | bytes 9437184 | tf_op jit(solution)/shard_map/psum | solution.py:132
  (153 shorter events, 30.6 us)
Async XLA Ops:
  0.0 12.4 %copy-start.4 = (s32[1,1,8]{2,1,0:T(1,128)S(1)}, s32[1,1,8]{2,1,0:T(1,128)}, u32[]{:S(2)}) copy-start(s32[1,1,8]{2,1,0:T(1,128)} %param.18) | copy-start | bytes 100
  0.0 13.8 %copy-start.3 = (s32[1,1,8,2]{2,3,1,0:T(2,128)S(1)}, s32[1,1,8,2]{2,3,1,0:T(2,128)}, u32[]{:S(2)}) copy-start(s32[1,1,8,2]{2,3,1,0:T(2,128)} %param.17) | copy-start | bytes 196
  0.0 45.0 %copy-start.1 = (s32[4,1,1,1,16,1]{4,5,3,2,1,0:T(1,128)S(1)}, s32[4,1,1,1,16,1]{4,5,3,2,1,0:T(1,128)}, u32[]{:S(2)}) copy-start(s32[4,1,1,1,16,1]{4,5,3,2,1,0:T(1,128)} %param.20) | copy-start | bytes 772
  0.0 46.7 %copy-start.2 = (s32[4,1,1,1,16]{4,3,2,1,0:T(1,128)S(1)}, s32[4,1,1,1,16]{4,3,2,1,0:T(1,128)}, u32[]{:S(2)}) copy-start(s32[4,1,1,1,16]{4,3,2,1,0:T(1,128)} %param.21) | copy-start | bytes 772
  0.0 64.3 %copy-start = (bf16[1,1,8,2,128,128]{5,4,3,2,1,0:T(8,128)(2,1)S(1)}, bf16[1,1,8,2,128,128]{5,4,3,2,1,0:T(8,128)(2,1)}, u32[]{:S(2)}) copy-start(bf16[1,1,8,2,128,128]{5,4,3,2,1,0:T(8,128)(2,1)} %param.16) | copy-start | bytes 1572868
  0.0 10.7 %collective-permute-start = (s32[8]{0:T(128)}, s32[8]{0:T(128)S(1)}, u32[]{:S(2)}, u32[]{:S(2)}) collective-permute-start(s32[8]{0:T(128)} %bitcast.190), channel_id=1, source_target_pairs={{0,14},{2,0},{4,2},{6,4},{8,6},{10,8},{12,10},{14,12},{1,15},{3,1}... | collective-permute-start | bytes 104 | tf_op jit(solution)/shard_map/ppermute | solution.py:19
  0.1 12.4 %collective-permute-start.2 = (s32[8,2]{0,1:T(2,128)}, s32[8,2]{0,1:T(2,128)S(1)}, u32[]{:S(2)}, u32[]{:S(2)}) collective-permute-start(s32[8,2]{0,1:T(2,128)} %bitcast.189), channel_id=1, source_target_pairs={{0,14},{2,0},{4,2},{6,4},{8,6},{10,8},{12,10},{14,12},{1,15},{3,1}... | collective-permute-start | bytes 200 | tf_op jit(solution)/shard_map/ppermute | solution.py:19
  5.1 39.8 %collective-permute-start.4 = (s32[4,16,1]{1,0,2:T(4,128)}, s32[4,16,1]{1,0,2:T(4,128)S(1)}, u32[]{:S(2)}, u32[]{:S(2)}) collective-permute-start(s32[4,16,1]{1,0,2:T(4,128)} %bitcast.185), channel_id=1, source_target_pairs={{0,16},{16,0},{1,17},{17,1},{2,18},{18,2},{3,19},{19,3},{4,20},{20... | collective-permute-start | bytes 776 | tf_op jit(solution)/shard_map/ppermute | solution.py:19
  6.7 40.0 %collective-permute-start.5 = (s32[4,16]{1,0:T(4,128)}, s32[4,16]{1,0:T(4,128)S(1)}, u32[]{:S(2)}, u32[]{:S(2)}) collective-permute-start(s32[4,16]{1,0:T(4,128)} %bitcast.187), channel_id=1, source_target_pairs={{0,16},{16,0},{1,17},{17,1},{2,18},{18,2},{3,19},{19,3},{4,20},{20... | collective-permute-start | bytes 776 | tf_op jit(solution)/shard_map/ppermute | solution.py:19
  7.2 57.2 %collective-permute-start.1 = (bf16[8,2,128,128]{3,2,1,0:T(8,128)(2,1)}, bf16[8,2,128,128]{3,2,1,0:T(8,128)(2,1)S(1)}, u32[]{:S(2)}, u32[]{:S(2)}) collective-permute-start(bf16[8,2,128,128]{3,2,1,0:T(8,128)(2,1)} %bitcast.176), channel_id=1, source_target_pairs={{0,14},{2,0},{4,2},{6,4},{8,6},{10,8},{12,10},{14,12},{1,15},{3,1}... | collective-permute-start | bytes 1572872 | tf_op jit(solution)/shard_map/ppermute | solution.py:19
  10.8 82.8 %collective-permute-start.3 = (bf16[4,16,1,128,128]{3,4,1,2,0:T(8,128)(2,1)S(1)}, bf16[4,16,1,128,128]{3,4,1,2,0:T(8,128)(2,1)}, u32[]{:S(2)}, u32[]{:S(2)}) collective-permute-start(bf16[4,16,1,128,128]{3,4,1,2,0:T(8,128)(2,1)S(1)} %bitcast.171), channel_id=1, source_target_pairs={{0,16},{16,0},{1,17},{17,1},{2,18},{18,2},{3,19},{19,3},{4,20},{20... | collective-permute-start | bytes 6291464 | tf_op jit(solution)/shard_map/ppermute | solution.py:19
  12.5 8.5 %collective-permute-start.6 = (s32[8]{0:T(128)S(1)}, s32[8]{0:T(128)S(1)}, u32[]{:S(2)}, u32[]{:S(2)}) collective-permute-start(s32[8]{0:T(128)S(1)} %broadcast_select_fusion.6), channel_id=1, source_target_pairs={{0,14},{2,0},{4,2},{6,4},{8,6},{10,8},{12,10},{14,12},{1,15},{3,1}... | collective-permute-start | bytes 104 | tf_op jit(solution)/shard_map/ppermute | solution.py:19
  21.0 4.5 %collective-permute-start.12 = (s32[8]{0:T(128)S(1)}, s32[8]{0:T(128)S(1)}, u32[]{:S(2)}, u32[]{:S(2)}) collective-permute-start(s32[8]{0:T(128)S(1)} %collective-permute-done.6), channel_id=1, source_target_pairs={{0,14},{2,0},{4,2},{6,4},{8,6},{10,8},{12,10},{14,12},{1,15},{3,1}... | collective-permute-start | bytes 104 | tf_op jit(solution)/shard_map/ppermute | solution.py:19
  25.5 4.5 %collective-permute-start.18 = (s32[8]{0:T(128)S(1)}, s32[8]{0:T(128)S(1)}, u32[]{:S(2)}, u32[]{:S(2)}) collective-permute-start(s32[8]{0:T(128)S(1)} %collective-permute-done.12), channel_id=1, source_target_pairs={{0,14},{2,0},{4,2},{6,4},{8,6},{10,8},{12,10},{14,12},{1,15},{3,1}... | collective-permute-start | bytes 104 | tf_op jit(solution)/shard_map/ppermute | solution.py:19
  30.0 4.5 %collective-permute-start.8 = (s32[8,2]{0,1:T(2,128)S(1)}, s32[8,2]{0,1:T(2,128)S(1)}, u32[]{:S(2)}, u32[]{:S(2)}) collective-permute-start(s32[8,2]{0,1:T(2,128)S(1)} %broadcast_select_fusion.5), channel_id=1, source_target_pairs={{0,14},{2,0},{4,2},{6,4},{8,6},{10,8},{12,10},{14,12},{1,15},{3,1}... | collective-permute-start | bytes 200 | tf_op jit(solution)/shard_map/ppermute | solution.py:19
  34.5 5.4 %collective-permute-start.14 = (s32[8,2]{0,1:T(2,128)S(1)}, s32[8,2]{0,1:T(2,128)S(1)}, u32[]{:S(2)}, u32[]{:S(2)}) collective-permute-start(s32[8,2]{0,1:T(2,128)S(1)} %collective-permute-done.8), channel_id=1, source_target_pairs={{0,14},{2,0},{4,2},{6,4},{8,6},{10,8},{12,10},{14,12},{1,15},{3,1}... | collective-permute-start | bytes 200 | tf_op jit(solution)/shard_map/ppermute | solution.py:19
  40.0 7.4 %collective-permute-start.20 = (s32[8,2]{0,1:T(2,128)S(1)}, s32[8,2]{0,1:T(2,128)S(1)}, u32[]{:S(2)}, u32[]{:S(2)}) collective-permute-start(s32[8,2]{0,1:T(2,128)S(1)} %collective-permute-done.14), channel_id=1, source_target_pairs={{0,14},{2,0},{4,2},{6,4},{8,6},{10,8},{12,10},{14,12},{1,15},{3,1}... | collective-permute-start | bytes 200 | tf_op jit(solution)/shard_map/ppermute | solution.py:19
  45.1 11.9 %collective-permute-start.10 = (s32[4,16,1]{1,0,2:T(4,128)S(1)}, s32[4,16,1]{1,0,2:T(4,128)S(1)}, u32[]{:S(2)}, u32[]{:S(2)}) collective-permute-start(s32[4,16,1]{1,0,2:T(4,128)S(1)} %fusion.62), channel_id=1, source_target_pairs={{0,16},{16,0},{1,17},{17,1},{2,18},{18,2},{3,19},{19,3},{4,20},{20... | collective-permute-start | bytes 776 | tf_op jit(solution)/shard_map/ppermute | solution.py:19
  46.8 11.8 %collective-permute-start.11 = (s32[4,16]{1,0:T(4,128)S(1)}, s32[4,16]{1,0:T(4,128)S(1)}, u32[]{:S(2)}, u32[]{:S(2)}) collective-permute-start(s32[4,16]{1,0:T(4,128)S(1)} %fusion.65), channel_id=1, source_target_pairs={{0,16},{16,0},{1,17},{17,1},{2,18},{18,2},{3,19},{19,3},{4,20},{20... | collective-permute-start | bytes 776 | tf_op jit(solution)/shard_map/ppermute | solution.py:19
  57.0 3.7 %collective-permute-start.16 = (s32[4,16,1]{1,0,2:T(4,128)S(1)}, s32[4,16,1]{1,0,2:T(4,128)S(1)}, u32[]{:S(2)}, u32[]{:S(2)}) collective-permute-start(s32[4,16,1]{1,0,2:T(4,128)S(1)} %constant_dynamic-slice_fusion.9), channel_id=1, source_target_pairs={{0,16},{16,0},{1,17},{17,1},{2,18},{18,2},{3,19},{19,3},{4,20},{20... | collective-permute-start | bytes 776 | tf_op jit(solution)/shard_map/ppermute | solution.py:19
  58.6 3.7 %collective-permute-start.17 = (s32[4,16]{1,0:T(4,128)S(1)}, s32[4,16]{1,0:T(4,128)S(1)}, u32[]{:S(2)}, u32[]{:S(2)}) collective-permute-start(s32[4,16]{1,0:T(4,128)S(1)} %constant_dynamic-slice_fusion.8), channel_id=1, source_target_pairs={{0,16},{16,0},{1,17},{17,1},{2,18},{18,2},{3,19},{19,3},{4,20},{20... | collective-permute-start | bytes 776 | tf_op jit(solution)/shard_map/ppermute | solution.py:19
  60.7 3.7 %collective-permute-start.22 = (s32[4,16,1]{1,0,2:T(4,128)S(1)}, s32[4,16,1]{1,0,2:T(4,128)S(1)}, u32[]{:S(2)}, u32[]{:S(2)}) collective-permute-start(s32[4,16,1]{1,0,2:T(4,128)S(1)} %constant_dynamic-slice_fusion.7), channel_id=1, source_target_pairs={{0,16},{16,0},{1,17},{17,1},{2,18},{18,2},{3,19},{19,3},{4,20},{20... | collective-permute-start | bytes 776 | tf_op jit(solution)/shard_map/ppermute | solution.py:19
  62.3 4.4 %collective-permute-start.23 = (s32[4,16]{1,0:T(4,128)S(1)}, s32[4,16]{1,0:T(4,128)S(1)}, u32[]{:S(2)}, u32[]{:S(2)}) collective-permute-start(s32[4,16]{1,0:T(4,128)S(1)} %constant_dynamic-slice_fusion.6), channel_id=1, source_target_pairs={{0,16},{16,0},{1,17},{17,1},{2,18},{18,2},{3,19},{19,3},{4,20},{20... | collective-permute-start | bytes 776 | tf_op jit(solution)/shard_map/ppermute | solution.py:19
  65.3 12.4 %collective-permute-start.7 = (bf16[8,2,128,128]{3,2,1,0:T(8,128)(2,1)S(1)}, bf16[8,2,128,128]{3,2,1,0:T(8,128)(2,1)S(1)}, u32[]{:S(2)}, u32[]{:S(2)}) collective-permute-start(bf16[8,2,128,128]{3,2,1,0:T(8,128)(2,1)S(1)} %get-tuple-element.279), channel_id=1, source_target_pairs={{0,14},{2,0},{4,2},{6,4},{8,6},{10,8},{12,10},{14,12},{1,15},{3,1}... | collective-permute-start | bytes 1572872 | tf_op jit(solution)/shard_map/ppermute | solution.py:19
  77.7 13.6 %collective-permute-start.13 = (bf16[8,2,128,128]{3,2,1,0:T(8,128)(2,1)S(1)}, bf16[8,2,128,128]{3,2,1,0:T(8,128)(2,1)S(1)}, u32[]{:S(2)}, u32[]{:S(2)}) collective-permute-start(bf16[8,2,128,128]{3,2,1,0:T(8,128)(2,1)S(1)} %collective-permute-done.7), channel_id=1, source_target_pairs={{0,14},{2,0},{4,2},{6,4},{8,6},{10,8},{12,10},{14,12},{1,15},{3,1}... | collective-permute-start | bytes 1572872 | tf_op jit(solution)/shard_map/ppermute | solution.py:19
  91.3 11.4 %collective-permute-start.19 = (bf16[8,2,128,128]{3,2,1,0:T(8,128)(2,1)S(1)}, bf16[8,2,128,128]{3,2,1,0:T(8,128)(2,1)S(1)}, u32[]{:S(2)}, u32[]{:S(2)}) collective-permute-start(bf16[8,2,128,128]{3,2,1,0:T(8,128)(2,1)S(1)} %collective-permute-done.13), channel_id=1, source_target_pairs={{0,14},{2,0},{4,2},{6,4},{8,6},{10,8},{12,10},{14,12},{1,15},{3,1}... | collective-permute-start | bytes 1572872 | tf_op jit(solution)/shard_map/ppermute | solution.py:19
  99.1 42.5 %collective-permute-start.9 = (bf16[4,16,1,128,128]{3,4,1,2,0:T(8,128)(2,1)}, bf16[4,16,1,128,128]{3,4,1,2,0:T(8,128)(2,1)}, u32[]{:S(2)}, u32[]{:S(2)}) collective-permute-start(bf16[4,16,1,128,128]{3,4,1,2,0:T(8,128)(2,1)} %fusion.43), channel_id=1, source_target_pairs={{0,16},{16,0},{1,17},{17,1},{2,18},{18,2},{3,19},{19,3},{4,20},{20... | collective-permute-start | bytes 6291464 | tf_op jit(solution)/shard_map/ppermute | solution.py:19
  147.4 38.5 %collective-permute-start.15 = (bf16[4,16,1,128,128]{3,4,1,2,0:T(8,128)(2,1)}, bf16[4,16,1,128,128]{3,4,1,2,0:T(8,128)(2,1)}, u32[]{:S(2)}, u32[]{:S(2)}) collective-permute-start(bf16[4,16,1,128,128]{3,4,1,2,0:T(8,128)(2,1)} %fusion.41), channel_id=1, source_target_pairs={{0,16},{16,0},{1,17},{17,1},{2,18},{18,2},{3,19},{19,3},{4,20},{20... | collective-permute-start | bytes 6291464 | tf_op jit(solution)/shard_map/ppermute | solution.py:19
  191.7 39.9 %collective-permute-start.21 = (bf16[4,16,1,128,128]{3,4,1,2,0:T(8,128)(2,1)}, bf16[4,16,1,128,128]{3,4,1,2,0:T(8,128)(2,1)}, u32[]{:S(2)}, u32[]{:S(2)}) collective-permute-start(bf16[4,16,1,128,128]{3,4,1,2,0:T(8,128)(2,1)} %fusion.40), channel_id=1, source_target_pairs={{0,16},{16,0},{1,17},{17,1},{2,18},{18,2},{3,19},{19,3},{4,20},{20... | collective-permute-start | bytes 6291464 | tf_op jit(solution)/shard_map/ppermute | solution.py:19
where the time goes:
time: 310 us; the launch traced here: 307 us
  local copies, waits for them, and re-layouts  89.5 us (29%)
  other arithmetic  79.5 us (26%)
  waiting for transfers between devices  53.2 us (17%)
  starting transfers between devices  37.2 us (12%)
  matrix products  26.8 us (9%)
  blocking collectives  20.3 us (7%)
    gather x16, local copies, waits for them, and re-layouts, one_group(): chosen = jnp.take(rows_dense, cols_part, axis=0)  68.8 us
    ppermute x24, waiting for transfers between devices, shifted(): return lax.ppermute(value, axis, pairs)  53.2 us
    convert_element_type x8, other arithmetic, dense_panel(): spread.astype(jnp.bfloat16)  39.5 us
    ppermute x24, starting transfers between devices, shifted(): return lax.ppermute(value, axis, pairs)  37.2 us
    dot_general x8, matrix products, one_group(): jnp.einsum('rtab,rtbn->ran', tiles_part, chosen, preferred_element_type=j...  26.8 us
    psum x1, blocking collectives, local(): summed = lax.psum(flat_running, 'depth')  20.3 us
    add x1, other arithmetic, local(): running = running + panel_product(tiles_a, cols_a, count_a, rows_dense)  13.8 us
    another operation x4, local copies, waits for them, and re-layouts  13.7 us
  transfers between devices with their start and end apart: 24, of which 10 were waited for; matrix products, arithmetic and copies ran while one was open for 42% of the time, Pallas kernels for 0%

commit v1 on v0

--- a/solution.py
+++ b/solution.py
@@ -1,8 +1,11 @@
+import functools
 import math
 
 import jax
 import jax.numpy as jnp
 from jax import lax
+from jax.experimental import pallas as pl
+from jax.experimental.pallas import tpu as pltpu
 from jax.sharding import PartitionSpec as P
 
 BC = 12
@@ -135,6 +138,260 @@
     return own_rows.astype(jnp.bfloat16)
 
 
+REACH = SHIFTS + 1
+MESH_ID = pl.DeviceIdType.MESH
+
+
+def gather_multiply(n_col, meta_ref, a_ref, b_ref, out_ref, A, B, M, run, MS, ktab, ptab, ltab,
+                    send_m, recv_m, send_a, recv_a, send_b, recv_b, local_sem):
+    row = lax.axis_index("row")
+    col = lax.axis_index("col")
+    dep = lax.axis_index("depth")
+    side = lax.rem(col, 2)
+    half = A.shape[2]
+    per_row = A.shape[3]
+    inner = B.shape[2]
+    size = B.shape[3]
+    out_cols = out_ref.shape[1] // size
+    terms = SHIFTS * 2 * per_row
+    zero_at = half * terms
+
+    def at(col_offset, flip_depth=False, flip_row=False):
+        return (
+            1 - row if flip_row else row,
+            lax.rem(col + col_offset + n_col, n_col),
+            1 - dep if flip_depth else dep,
+        )
+
+    chain_dev = at(-2)
+    twin_dev = at(0, True)
+    row_dev = at(0, False, True)
+    side_dev = (row, col + 1 - 2 * side, dep)
+
+    barrier = pltpu.get_barrier_semaphore()
+    reach = REACH - 1
+    offsets = [o for o in range(1, n_col) if o <= reach or n_col - o <= reach]
+    peers = [at(o, flip) for o in offsets for flip in (False, True)]
+    peers += [twin_dev, row_dev, at(0, True, True)]
+    for peer in peers:
+        pl.semaphore_signal(barrier, inc=1, device_id=peer, device_id_type=MESH_ID)
+    pl.semaphore_wait(barrier, len(peers))
+
+    def remote(src, dst, ssem, rsem, dev):
+        return pltpu.make_async_remote_copy(
+            src_ref=src, dst_ref=dst, send_sem=ssem, recv_sem=rsem, device_id=dev, device_id_type=MESH_ID
+        )
+
+    meta_copies = []
+    for q in range(REACH):
+        for d in range(2):
+            slot = q * 2 + d
+            if slot:
+                meta_copies.append(
+                    remote(meta_ref, M.at[slot], send_m.at[slot], recv_m.at[slot], at(-q, d == 1))
+                )
+    for d in range(2):
+        slot = REACH * 2 + d
+        meta_copies.append(
+            remote(meta_ref, M.at[slot], send_m.at[slot], recv_m.at[slot], at(0, d == 1, True))
+        )
+    for copy in meta_copies:
+        copy.start()
+    meta_local = pltpu.make_async_copy(meta_ref, M.at[0], local_sem.at[0])
+    meta_local.start()
+
+    own_a = a_ref.at[pl.ds(dep * half, half)]
+    swap = remote(a_ref.at[pl.ds((1 - dep) * half, half)], A.at[0, 1], send_a.at[0], recv_a.at[0, 1], twin_dev)
+    chain = [
+        remote(src, A.at[2, d], send_a.at[1 + d], recv_a.at[2, d], chain_dev)
+        for d, src in enumerate((own_a, A.at[0, 1]))
+    ]
+    chain2 = [
+        remote(A.at[2, d], A.at[4, d], send_a.at[3 + d], recv_a.at[4, d], chain_dev) for d in range(2)
+    ]
+    odd1 = [
+        remote(src, A.at[1, d], send_a.at[5 + d], recv_a.at[1, d], side_dev)
+        for d, src in enumerate((own_a, A.at[0, 1]))
+    ]
+    odd3 = [remote(A.at[2, d], A.at[3, d], send_a.at[7 + d], recv_a.at[3, d], side_dev) for d in range(2)]
+    even1 = [remote(A.at[2, d], A.at[1, d], send_a.at[5 + d], recv_a.at[1, d], side_dev) for d in range(2)]
+    even3 = [remote(A.at[4, d], A.at[3, d], send_a.at[7 + d], recv_a.at[3, d], side_dev) for d in range(2)]
+    a_local = pltpu.make_async_copy(own_a, A.at[0, 0], local_sem.at[1])
+
+    far_b, near_b, pass_b, b_local = [], [], [], []
+    for k in range(SHIFTS // 2):
+        s_far = lax.rem(col + 1, 2) + 2 * k
+        m_far = lax.rem(1 - row + col + s_far, n_col) // 2
+        far_b.append(remote(b_ref.at[m_far], B.at[0, s_far], send_b.at[k], recv_b.at[0, s_far], row_dev))
+        s_near = side + 2 * k
+        m_near = lax.rem(row + col + s_near, n_col) // 2
+        near_b.append(remote(b_ref.at[m_near], B.at[1, s_near], send_b.at[2 + k], recv_b.at[1, s_near], twin_dev))
+        b_local.append(pltpu.make_async_copy(b_ref.at[m_near], B.at[0, s_near], local_sem.at[2 + k]))
+        pass_b.append(remote(B.at[0, s_far], B.at[1, s_far], send_b.at[4 + k], recv_b.at[1, s_far], twin_dev))
+
+    swap.start()
+    chain[0].start()
+    far_b[0].start()
+
+    @pl.when(side == 1)
+    def _():
+        odd1[0].start()
+
+    far_b[1].start()
+    for copy in near_b:
+        copy.start()
+    a_local.start()
+    for copy in b_local:
+        copy.start()
+
+    swap.wait_recv()
+    chain[1].start()
+
+    @pl.when(side == 1)
+    def _():
+        odd1[1].start()
+
+    run[zero_at] = jnp.zeros(run.shape[1:], jnp.float32)
+    meta_local.wait()
+    for copy in meta_copies:
+        copy.wait_recv()
+    to_scalars = pltpu.make_async_copy(M, MS, local_sem.at[4])
+    to_scalars.start()
+    to_scalars.wait()
+
+    def tables(r, carry):
+        cs = []
+        for s in range(SHIFTS):
+            slot_b = lax.rem(row + col + s, n_col) // 2
+            near = lax.rem(col + s, 2) == 0
+            for d in range(2):
+                m_at = jnp.where(near, d, REACH * 2 + d)
+                for t in range(per_row):
+                    k = MS[(s + row) * 2 + d, 0, (dep * half + r) * per_row + t]
+                    kk = jnp.maximum(k, 0)
+                    c = MS[m_at, 0, 2 * half * per_row + slot_b * inner + kk]
+                    c = jnp.where(k >= 0, c, -1)
+                    here = r * terms + len(cs)
+                    before = jnp.int32(zero_at)
+                    for at_p, c_p in enumerate(cs):
+                        before = jnp.where(c_p == c, r * terms + at_p, before)
+                    ktab[here] = kk
+                    ptab[here] = before
+                    cs.append(c)
+        for c in range(out_cols):
+            last = jnp.int32(zero_at)
+            for at_p, c_p in enumerate(cs):
+                last = jnp.where(c_p == c, r * terms + at_p, last)
+            ltab[r * out_cols + c] = last
+        return carry
+
+    lax.fori_loop(0, half, tables, 0)
+
+    for d in range(2):
+        chain[d].wait_recv()
+        chain2[d].start()
+
+        @pl.when(side == 0)
+        def _():
+            even1[d].start()
+
+        @pl.when(side == 1)
+        def _():
+            odd3[d].start()
+
+    far_b[0].wait_recv()
+    pass_b[0].start()
+    for d in range(2):
+        chain2[d].wait_recv()
+
+        @pl.when(side == 0)
+        def _():
+            even3[d].start()
+
+    far_b[1].wait_recv()
+    pass_b[1].start()
+
+    a_local.wait()
+    for copy in b_local:
+        copy.wait()
+    for copy in near_b:
+        copy.wait_recv()
+    for d in range(2):
+        odd1[d].wait_recv()
+    for copy in pass_b:
+        copy.wait_recv()
+    for d in range(2):
+        odd3[d].wait_recv()
+
+    def products(step, carry):
+        s = step // 2
+        d = lax.rem(step, 2)
+        for t in range(per_row):
+            for r in range(half):
+                here = r * terms + step * per_row + t
+                value = jnp.dot(
+                    A[s + row, d, r, t], B[d, s, ktab[here]], preferred_element_type=jnp.float32
+                )
+                run[here] = value + run[ptab[here]]
+        return carry
+
+    lax.fori_loop(0, SHIFTS * 2, products, 0)
+
+    def place(r, carry):
+        rows = pl.ds(pl.multiple_of(r * size, size), size)
+        for c in range(out_cols):
+            out_ref[rows, c * size : (c + 1) * size] = run[ltab[r * out_cols + c]].astype(out_ref.dtype)
+        return carry
+
+    lax.fori_loop(0, half, place, 0)
+
+    for copy in meta_copies + [swap] + chain + chain2 + odd1 + odd3 + far_b + near_b + pass_b:
+        copy.wait_send()
+
+
+def local_fast(n_col, a_tiles, a_cols, a_count, b_tiles, b_cols, b_count):
+    block_rows, per_row, size = a_tiles.shape[2:5]
+    slots, inner = b_tiles.shape[0], b_tiles.shape[4]
+    half = block_rows // 2
+    t_ids = lax.broadcasted_iota(jnp.int32, (block_rows, per_row), 1)
+    a_meta = jnp.where(t_ids < a_count.reshape(block_rows, 1), a_cols.reshape(block_rows, per_row), -1)
+    b_meta = jnp.where(b_count.reshape(slots * inner) > 0, b_cols.reshape(slots * inner), -1)
+    flat = jnp.concatenate([a_meta.reshape(-1), b_meta])
+    width = -(-flat.shape[0] // 128) * 128
+    meta = jnp.broadcast_to(jnp.pad(flat, (0, width - flat.shape[0]))[None, :], (8, width))
+    terms = SHIFTS * 2 * per_row
+    count = half * terms
+    metas = REACH * 2 + 2
+    any_spec = pl.BlockSpec(memory_space=pl.ANY)
+    vmem_spec = pl.BlockSpec(memory_space=pltpu.VMEM)
+    return pl.pallas_call(
+        functools.partial(gather_multiply, n_col),
+        out_shape=jax.ShapeDtypeStruct((half * size, BC * size), jnp.bfloat16),
+        in_specs=[vmem_spec, any_spec, any_spec],
+        out_specs=vmem_spec,
+        scratch_shapes=[
+            pltpu.VMEM((REACH, 2, half, per_row, size, size), jnp.bfloat16),
+            pltpu.VMEM((2, SHIFTS, inner, size, size), jnp.bfloat16),
+            pltpu.VMEM((metas, 8, width), jnp.int32),
+            pltpu.VMEM((count + 1, size, size), jnp.float32),
+            pltpu.SMEM((metas, 8, width), jnp.int32),
+            pltpu.SMEM((count,), jnp.int32),
+            pltpu.SMEM((count,), jnp.int32),
+            pltpu.SMEM((half * BC,), jnp.int32),
+            pltpu.SemaphoreType.DMA((metas,)),
+            pltpu.SemaphoreType.DMA((metas,)),
+            pltpu.SemaphoreType.DMA((9,)),
+            pltpu.SemaphoreType.DMA((REACH, 2)),
+            pltpu.SemaphoreType.DMA((6,)),
+            pltpu.SemaphoreType.DMA((2, SHIFTS)),
+            pltpu.SemaphoreType.DMA((5,)),
+        ],
+        compiler_params=pltpu.CompilerParams(
+            collective_id=0, has_side_effects=True, vmem_limit_bytes=40 * 1024 * 1024
+        ),
+    )(meta, a_tiles.reshape(block_rows, per_row, size, size), b_tiles.reshape(slots, inner, size, size))
+
+
 def solution(mesh):
     placed = (
         P("row", ("col", "depth"), None, None, None, None),
@@ -144,6 +401,11 @@
         P(None, "row", "depth", "col", None, None),
         P(None, "row", "depth", "col", None),
     )
+    n_col = mesh.shape["col"]
+    if mesh.shape["row"] == 2 and mesh.shape["depth"] == 2 and n_col % 2 == 0 and n_col > SHIFTS:
+        body = functools.partial(local_fast, n_col)
+    else:
+        body = local
     return jax.shard_map(
-        local, mesh=mesh, in_specs=placed, out_specs=P(("row", "depth"), "col"), check_vma=False
+        body, mesh=mesh, in_specs=placed, out_specs=P(("row", "depth"), "col"), check_vma=False
     )

time: 310 us -> 47.2 us (0.15)
  local copies, waits for them, and re-layouts: 89.5 us -> 5.4 us
  other arithmetic: 79.5 us -> 2.87 us
  waiting for transfers between devices: 53.2 us -> 0 us
  Pallas kernels: 0 us -> 38.7 us
  starting transfers between devices: 37.2 us -> 0 us
  matrix products: 26.8 us -> 0 us
  blocking collectives: 20.3 us -> 0 us
    gather x16 -> x0, local copies, waits for them, and re-layouts: 68.8 us -> none  [one_group(): chosen = jnp.take(rows_dense, cols_part, axis=0)]
    ppermute x24 -> x0, waiting for transfers between devices: 53.2 us -> none  [shifted(): return lax.ppermute(value, axis, pairs)]
    convert_element_type x8 -> x0, other arithmetic: 39.5 us -> none  [dense_panel(): spread.astype(jnp.bfloat16)]
    pallas_call x0 -> x1, Pallas kernels: none -> 38.7 us  [local_fast(): pl.pallas_call(functools.partial(gather_multiply, n_col), out_shape=jax.S...]
    ppermute x24 -> x0, starting transfers between devices: 37.2 us -> none  [shifted(): return lax.ppermute(value, axis, pairs)]
    dot_general x8 -> x0, matrix products: 26.8 us -> none  [one_group(): jnp.einsum('rtab,rtbn->ran', tiles_part, chosen, preferred_element_type=j...]
    psum x1 -> x0, blocking collectives: 20.3 us -> none  [local(): summed = lax.psum(flat_running, 'depth')]
    add x1 -> x0, other arithmetic: 13.8 us -> none  [local(): running = running + panel_product(tiles_a, cols_a, count_a, rows_dense)]
  transfers between devices with their start and end apart: 24 -> 0, of which waited for: 10 -> 0; matrix products, arithmetic and copies ran while one was open for 42% -> 0% of each run, Pallas kernels for 0% -> 0%
where the time goes in v1:
time: 47.2 us; the launch traced here: 47 us
  Pallas kernels  38.7 us (82%)
  local copies, waits for them, and re-layouts  5.4 us (11%)
  other arithmetic  2.87 us (6%)
    pallas_call x1, Pallas kernels, local_fast(): pl.pallas_call(functools.partial(gather_multiply, n_col), out_shape=jax.S...  38.7 us
    unnamed x7, local copies, waits for them, and re-layouts  5.05 us
    unnamed x1, other arithmetic  1.34 us

profile of v1, /device:TPU:2, one launch (start us, length us, event | category | flops | bytes accessed | tf_op | source)
XLA Modules:
  0.0 47.0 jit_solution(10506595910196265329)
XLA Ops:
  0.0 0.7 %compare_reduce_fusion = pred[4,16]{1,0:T(4,128)(4,1)S(1)} fusion(s32[4,1,1,1,16]{4,3,2,1,0:T(1,128)} %param.11), kind=kLoop, calls=%fused_computation | loop fusion | flops 64 | bytes 320 | tf_op jit(solution)/shard_map/gt | solution.py:358
  0.7 0.1 gt.11
  0.8 0.7 %iota_compare_fusion = pred[8,2]{1,0:T(8,128)(4,1)S(1)} fusion(s32[8]{0:T(128)} %bitcast.8), kind=kLoop, calls=%fused_computation.1 | loop fusion | flops 16 | bytes 48 | tf_op jit(solution)/shard_map/lt | solution.py:357
  1.5 0.1 lt.17
  1.6 0.5 %broadcast.13 = s32[]{:T(128)} broadcast(s32[]{:T(128)} %constant.0.clone.1), dimensions={} | broadcast | bytes 8 | tf_op args[4]
  2.1 1.3 %reduce.5 = s32[4,16]{1,0:T(4,128)S(1)} reduce(s32[4,1,1,1,16,1]{4,5,3,2,1,0:T(1,128)} %param.10, s32[]{:T(128)} %broadcast.13), dimensions={1,2,3,5}, to_apply=%param.10.reduce_sub_computation.3 | reduce | bytes 516 | tf_op args[4]
  3.5 0.1 reshape.24
  3.6 0.8 %copy.8 = s32[1,1,8,2]{3,2,1,0:T(8,128)S(1)} copy(s32[1,1,8,2]{2,3,1,0:T(2,128)} %param.7) | data formatting | bytes 128 | tf_op args[1]
  4.3 0.1 reshape.23
  4.4 0.1 pad_add_fusion
  4.5 0.0 copy-start
  4.5 1.6 %copy-done = bf16[4,1,1,1,16,1,128,128]{7,6,5,4,3,2,1,0:T(8,128)(2,1)S(1)} copy-done((bf16[4,1,1,1,16,1,128,128]{7,6,5,4,3,2,1,0:T(8,128)(2,1)S(1)}, bf16[4,1,1,1,16,1,128,128]{7,6,5,4,3,2,1,0:T(8,128)(2,1)}, u32[]{:S(2)}) %copy-start) | copy-done | bytes 2097176
  6.1 0.0 copy-start.1
  6.1 1.0 %copy-done.1 = bf16[1,1,8,2,128,128]{5,4,3,2,1,0:T(8,128)(2,1)S(1)} copy-done((bf16[1,1,8,2,128,128]{5,4,3,2,1,0:T(8,128)(2,1)S(1)}, bf16[1,1,8,2,128,128]{5,4,3,2,1,0:T(8,128)(2,1)}, u32[]{:S(2)}) %copy-start.1) | copy-done | bytes 524312
  7.1 38.7 %shard_map.64 = bf16[512,1536]{1,0:T(8,128)(2,1)S(1)} custom-call(s32[8,128]{1,0:T(8,128)S(1)} %broadcast_in_dim.16.meta_ref, bf16[8,2,128,128]{3,2,1,0:T(8,128)(2,1)S(1)} %bitcast.7, bf16[4,16,128,128]{3,2,1,0:T(8,128)(2,1)S(1)} %bitcast.6), custom_call_target="tpu_custom_call" | custom-call | tf_op jit(solution)/shard_map/pallas_call | solution.py:367
  45.8 1.1 %copy.10 = bf16[512,1536]{1,0:T(8,128)(2,1)} copy(bf16[512,1536]{1,0:T(8,128)(2,1)S(1)} %shard_map.64) | data formatting | bytes 3145728
  (4 shorter events, 0.0 us)
Async XLA Ops:
  4.5 1.6 %copy-start = (bf16[4,1,1,1,16,1,128,128]{7,6,5,4,3,2,1,0:T(8,128)(2,1)S(1)}, bf16[4,1,1,1,16,1,128,128]{7,6,5,4,3,2,1,0:T(8,128)(2,1)}, u32[]{:S(2)}) copy-start(bf16[4,1,1,1,16,1,128,128]{7,6,5,4,3,2,1,0:T(8,128)(2,1)} %param.9) | copy-start | bytes 6291460
  6.1 1.0 %copy-start.1 = (bf16[1,1,8,2,128,128]{5,4,3,2,1,0:T(8,128)(2,1)S(1)}, bf16[1,1,8,2,128,128]{5,4,3,2,1,0:T(8,128)(2,1)}, u32[]{:S(2)}) copy-start(bf16[1,1,8,2,128,128]{5,4,3,2,1,0:T(8,128)(2,1)} %param.6) | copy-start | bytes 1572868

commit v2 on v0

--- a/solution.py
+++ b/solution.py
@@ -1,8 +1,11 @@
+import functools
 import math
 
 import jax
 import jax.numpy as jnp
 from jax import lax
+from jax.experimental import pallas as pl
+from jax.experimental.pallas import tpu as pltpu
 from jax.sharding import PartitionSpec as P
 
 BC = 12
@@ -135,6 +138,327 @@
     return own_rows.astype(jnp.bfloat16)
 
 
+REACH = SHIFTS + 1
+CHUNKS = 4
+MESH_ID = pl.DeviceIdType.MESH
+
+
+def gather_multiply(n_col, a_cols, a_count, b_cols, b_count, a_ref, b_ref, out_ref, A, Bn0, Bn1, Bf0, Bf1,
+                    Gn0, Gn1, Gf0, Gf1, MA, MC, MB, MK, SA, SC, SB, SK, run, ktab, ptab, ltab,
+                    send_m, recv_m, send_a, recv_a, send_b, recv_b, local_sem):
+    row = lax.axis_index("row")
+    col = lax.axis_index("col")
+    dep = lax.axis_index("depth")
+    side = lax.rem(col, 2)
+    half = A.shape[2]
+    per_row = A.shape[3]
+    size = A.shape[4]
+    inner = Bn0.shape[0]
+    out_cols = out_ref.shape[1] // size
+    terms = SHIFTS * 2 * per_row
+    zero_at = half * terms
+    units = [(d, r) for d in range(2) for r in range(half)]
+    count_u = len(units)
+    step_b = inner // CHUNKS
+
+    def at(col_offset, flip_depth=False, flip_row=False):
+        return (
+            1 - row if flip_row else row,
+            lax.rem(col + col_offset + n_col, n_col),
+            1 - dep if flip_depth else dep,
+        )
+
+    chain_dev = at(-2)
+    twin_dev = at(0, True)
+    row_dev = at(0, False, True)
+    side_dev = (row, col + 1 - 2 * side, dep)
+
+    def remote(src, dst, ssem, rsem, dev):
+        return pltpu.make_async_remote_copy(
+            src_ref=src, dst_ref=dst, send_sem=ssem, recv_sem=rsem, device_id=dev, device_id_type=MESH_ID
+        )
+
+    s_near = [side + 2 * k for k in range(2)]
+    s_far = [1 - side + 2 * k for k in range(2)]
+    m_near = [lax.rem(row + col + s, n_col) // 2 for s in s_near]
+    m_far = [lax.rem(1 - row + col + s, n_col) // 2 for s in s_far]
+    m_mine = [lax.rem(row + col + s, n_col) // 2 for s in s_far]
+    near_own, near_twin = (Bn0, Bn1), (Gn0, Gn1)
+    far_own, far_twin = (Bf0, Bf1), (Gf0, Gf1)
+    index_local = [
+        pltpu.make_async_copy(src, dst.at[0], local_sem.at[n])
+        for n, (src, dst) in enumerate(((a_cols, MA), (a_count, MC), (b_cols, MB), (b_count, MK)))
+    ]
+    b_local = [pltpu.make_async_copy(b_ref.at[m_near[k]], near_own[k], local_sem.at[4 + k]) for k in range(2)]
+    a_local = pltpu.make_async_copy(a_ref.at[pl.ds(dep * half, half)], A.at[0, 0], local_sem.at[6])
+    for copy in index_local + b_local + [a_local]:
+        copy.start()
+
+    barrier = pltpu.get_barrier_semaphore()
+    reach = REACH - 1
+    offsets = [o for o in range(1, n_col) if o <= reach or n_col - o <= reach]
+    peers = [at(o, flip) for o in offsets for flip in (False, True)]
+    peers += [twin_dev, row_dev, at(0, True, True)]
+    for peer in peers:
+        pl.semaphore_signal(barrier, inc=1, device_id=peer, device_id_type=MESH_ID)
+    pl.semaphore_wait(barrier, len(peers))
+
+    index_copies = []
+    for q in range(REACH):
+        for d in range(2):
+            slot = q * 2 + d
+            if slot:
+                for n, (src, dst) in enumerate(((a_cols, MA), (a_count, MC))):
+                    index_copies.append(
+                        remote(src, dst.at[slot], send_m.at[n, slot], recv_m.at[n, slot], at(-q, d == 1))
+                    )
+    for slot in range(1, 4):
+        for n, (src, dst) in enumerate(((b_cols, MB), (b_count, MK))):
+            index_copies.append(
+                remote(
+                    src, dst.at[slot], send_m.at[2 + n, slot], recv_m.at[2 + n, slot],
+                    at(0, slot % 2 == 1, slot >= 2),
+                )
+            )
+
+    swap = [
+        remote(a_ref.at[(1 - dep) * half + r], A.at[0, 1, r], send_a.at[0, r], recv_a.at[0, half + r], twin_dev)
+        for r in range(half)
+    ]
+    first = [a_ref.at[dep * half + r] for r in range(half)] + [A.at[0, 1, r] for r in range(half)]
+
+    def to_panel(p, sources, send_row, dev):
+        return [
+            remote(src, A.at[p, d, r], send_a.at[send_row, u], recv_a.at[p, u], dev)
+            for u, ((d, r), src) in enumerate(zip(units, sources))
+        ]
+
+    def panel(p):
+        return [A.at[p, d, r] for d, r in units]
+
+    chain = to_panel(2, first, 1, chain_dev)
+    chain2 = to_panel(4, panel(2), 2, chain_dev)
+    odd1 = to_panel(1, first, 3, side_dev)
+    odd3 = to_panel(3, panel(2), 4, side_dev)
+    even1 = to_panel(1, panel(2), 3, side_dev)
+    even3 = to_panel(3, panel(4), 4, side_dev)
+
+    near_b = [
+        remote(b_ref.at[m_near[k]], near_twin[k], send_b.at[2 * k, CHUNKS], recv_b.at[2 * k, CHUNKS], twin_dev)
+        for k in range(2)
+    ]
+    far_b, pass_b = [], []
+    for k in range(2):
+        for c in range(CHUNKS):
+            part = pl.ds(c * step_b, step_b)
+            far_b.append(
+                remote(
+                    b_ref.at[m_far[k], part], far_own[k].at[part],
+                    send_b.at[2 * k, c], recv_b.at[2 * k, c], row_dev,
+                )
+            )
+            pass_b.append(
+                remote(
+                    far_own[k].at[part], far_twin[k].at[part],
+                    send_b.at[2 * k + 1, c], recv_b.at[2 * k + 1, c], twin_dev,
+                )
+            )
+
+    for copy in index_copies[:2] + index_copies[-6:]:
+        copy.start()
+    for copy in index_copies[2:-6]:
+        copy.start()
+    for r in range(half):
+        chain[r].start()
+        swap[r].start()
+
+        @pl.when(side == 1)
+        def _():
+            odd1[r].start()
+
+    for copy in far_b:
+        copy.start()
+    for copy in near_b:
+        copy.start()
+    run[zero_at] = jnp.zeros(run.shape[1:], jnp.float32)
+    for r in range(half):
+        swap[r].wait_recv()
+        chain[half + r].start()
+
+        @pl.when(side == 1)
+        def _():
+            odd1[half + r].start()
+
+    groups = [(s, m, k, d, far) for k in range(2) for far, s, m in ((0, s_near[k], m_near[k]), (1, s_far[k], m_mine[k]))
+              for d in range(2)]
+
+    def tables(r, carry):
+        cs = []
+        for s, m, _, d, far in groups:
+            slot = (s + row) * 2 + d
+            used = SC[slot, 0, dep * half + r]
+            for t in range(per_row):
+                k = SA[slot, t, dep * half + r]
+                c = SB[2 * far + d, m, 0, k]
+                ok = jnp.logical_and(used > t, SK[2 * far + d, m, 0, k] > 0)
+                c = jnp.where(ok, c, -1)
+                here = r * terms + len(cs)
+                before = jnp.int32(zero_at)
+                for at_p, c_p in enumerate(cs):
+                    before = jnp.where(c_p == c, r * terms + at_p, before)
+                ktab[here] = k
+                ptab[here] = before
+                cs.append(c)
+        for c in range(out_cols):
+            last = jnp.int32(zero_at)
+            for at_p, c_p in enumerate(cs):
+                last = jnp.where(c_p == c, r * terms + at_p, last)
+            ltab[r * out_cols + c] = last
+        return carry
+
+    def product(g, d, r, t, right):
+        here = r * terms + g * per_row + t
+        value = jnp.dot(A[groups[g][0] + row, d, r, t], right[ktab[here]], preferred_element_type=jnp.float32)
+        run[here] = value + run[ptab[here]]
+
+    def whole_group(g, right):
+        d = groups[g][3]
+
+        def one(t, carry):
+            for r in range(half):
+                product(g, d, r, t, right)
+            return carry
+
+        lax.fori_loop(0, per_row, one, 0)
+
+    for u in range(count_u):
+        chain[u].wait_recv()
+        chain2[u].start()
+
+        @pl.when(side == 0)
+        def _():
+            even1[u].start()
+
+        @pl.when(side == 1)
+        def _():
+            odd3[u].start()
+
+        if u % 2 == 1 and u // 2 < CHUNKS:
+            far_b[u // 2].wait_recv()
+            pass_b[u // 2].start()
+        if u == 1:
+            for copy in index_local:
+                copy.wait()
+            for copy in index_copies:
+                copy.wait_recv()
+            scalars = [
+                pltpu.make_async_copy(src, dst, local_sem.at[n])
+                for n, (src, dst) in enumerate(((MA, SA), (MC, SC), (MB, SB), (MK, SK)))
+            ]
+            for copy in scalars:
+                copy.start()
+            for copy in scalars:
+                copy.wait()
+        if 2 <= u < 2 + half:
+            tables(u - 2, 0)
+
+    def near_unit(u):
+        odd3[u].wait_recv()
+        d, r = units[u]
+        for t in range(per_row):
+            product(4 + d, d, r, t, (Bn1, Gn1)[d])
+
+    done = 0
+    for u in range(count_u):
+        chain2[u].wait_recv()
+
+        @pl.when(side == 0)
+        def _():
+            even3[u].start()
+
+        if u % 2 == 1 and u // 2 < CHUNKS:
+            far_b[CHUNKS + u // 2].wait_recv()
+            pass_b[CHUNKS + u // 2].start()
+        if u == 2:
+            a_local.wait()
+            for copy in b_local:
+                copy.wait()
+            for copy in near_b:
+                copy.wait_recv()
+            for copy in odd1:
+                copy.wait_recv()
+            for c in range(CHUNKS):
+                pass_b[c].wait_recv()
+        if 2 <= u < 6:
+            whole_group(u - 2, (Bn0, Gn0, Bf0, Gf0)[u - 2])
+        if u >= 5:
+            near_unit(done)
+            done += 1
+    for u in range(done, count_u):
+        near_unit(u)
+    whole_group(6, Bf1)
+    for c in range(CHUNKS):
+        pass_b[CHUNKS + c].wait_recv()
+    whole_group(7, Gf1)
+
+    def place(r, carry):
+        rows = pl.ds(pl.multiple_of(r * size, size), size)
+        for c in range(out_cols):
+            out_ref[rows, c * size : (c + 1) * size] = run[ltab[r * out_cols + c]].astype(out_ref.dtype)
+        return carry
+
+    lax.fori_loop(0, half, place, 0)
+
+    for copy in index_copies + swap + chain + chain2 + odd1 + odd3 + far_b + near_b + pass_b:
+        copy.wait_send()
+
+
+def local_fast(n_col, a_tiles, a_cols, a_count, b_tiles, b_cols, b_count):
+    block_rows, per_row, size = a_tiles.shape[2:5]
+    slots, inner = b_tiles.shape[0], b_tiles.shape[4]
+    half = block_rows // 2
+    terms = SHIFTS * 2 * per_row
+    count = half * terms
+    panels = REACH * 2
+    hbm = pl.BlockSpec(memory_space=pltpu.HBM)
+    vmem = pl.BlockSpec(memory_space=pltpu.VMEM)
+    index_shapes = [(panels, per_row, block_rows), (panels, 1, block_rows), (4, slots, 1, inner), (4, slots, 1, inner)]
+    right = pltpu.VMEM((inner, size, size), jnp.bfloat16)
+    return pl.pallas_call(
+        functools.partial(gather_multiply, n_col),
+        out_shape=jax.ShapeDtypeStruct((half * size, BC * size), jnp.bfloat16),
+        in_specs=[hbm] * 6,
+        out_specs=vmem,
+        scratch_shapes=[pltpu.VMEM((REACH, 2, half, per_row, size, size), jnp.bfloat16)]
+        + [right] * 8
+        + [pltpu.VMEM(shape, jnp.int32) for shape in index_shapes]
+        + [pltpu.SMEM(shape, jnp.int32) for shape in index_shapes]
+        + [
+            pltpu.VMEM((count + 1, size, size), jnp.float32),
+            pltpu.SMEM((count,), jnp.int32),
+            pltpu.SMEM((count,), jnp.int32),
+            pltpu.SMEM((half * BC,), jnp.int32),
+            pltpu.SemaphoreType.DMA((4, panels)),
+            pltpu.SemaphoreType.DMA((4, panels)),
+            pltpu.SemaphoreType.DMA((5, 2 * half)),
+            pltpu.SemaphoreType.DMA((REACH, 2 * half)),
+            pltpu.SemaphoreType.DMA((4, CHUNKS + 1)),
+            pltpu.SemaphoreType.DMA((4, CHUNKS + 1)),
+            pltpu.SemaphoreType.DMA((7,)),
+        ],
+        compiler_params=pltpu.CompilerParams(
+            collective_id=0, has_side_effects=True, vmem_limit_bytes=65200000
+        ),
+    )(
+        jnp.swapaxes(a_cols.reshape(block_rows, per_row), 0, 1),
+        a_count.reshape(1, block_rows),
+        b_cols.reshape(slots, 1, inner),
+        b_count.reshape(slots, 1, inner),
+        a_tiles.reshape(block_rows, per_row, size, size),
+        b_tiles.reshape(slots, inner, size, size),
+    )
+
+
 def solution(mesh):
     placed = (
         P("row", ("col", "depth"), None, None, None, None),
@@ -144,6 +468,11 @@
         P(None, "row", "depth", "col", None, None),
         P(None, "row", "depth", "col", None),
     )
+    n_col = mesh.shape["col"]
+    if mesh.shape["row"] == 2 and mesh.shape["depth"] == 2 and n_col % 2 == 0 and n_col > SHIFTS:
+        body = functools.partial(local_fast, n_col)
+    else:
+        body = local
     return jax.shard_map(
-        local, mesh=mesh, in_specs=placed, out_specs=P(("row", "depth"), "col"), check_vma=False
-    )
+        body, mesh=mesh, in_specs=placed, out_specs=P(("row", "depth"), "col"), check_vma=False
+    )

time: 310 us -> 39.4 us (0.13)
  local copies, waits for them, and re-layouts: 89.5 us -> 2.65 us
  other arithmetic: 79.5 us -> 0 us
  waiting for transfers between devices: 53.2 us -> 0 us
  starting transfers between devices: 37.2 us -> 0 us
  Pallas kernels: 0 us -> 36.6 us
  matrix products: 26.8 us -> 0 us
  blocking collectives: 20.3 us -> 0 us
    gather x16 -> x0, local copies, waits for them, and re-layouts: 68.8 us -> none  [one_group(): chosen = jnp.take(rows_dense, cols_part, axis=0)]
    ppermute x24 -> x0, waiting for transfers between devices: 53.2 us -> none  [shifted(): return lax.ppermute(value, axis, pairs)]
    convert_element_type x8 -> x0, other arithmetic: 39.5 us -> none  [dense_panel(): spread.astype(jnp.bfloat16)]
    ppermute x24 -> x0, starting transfers between devices: 37.2 us -> none  [shifted(): return lax.ppermute(value, axis, pairs)]
    pallas_call x0 -> x1, Pallas kernels: none -> 36.6 us  [local_fast(): pl.pallas_call(functools.partial(gather_multiply, n_col), out_shape=jax.S...]
    dot_general x8 -> x0, matrix products: 26.8 us -> none  [one_group(): jnp.einsum('rtab,rtbn->ran', tiles_part, chosen, preferred_element_type=j...]
    psum x1 -> x0, blocking collectives: 20.3 us -> none  [local(): summed = lax.psum(flat_running, 'depth')]
    add x1 -> x0, other arithmetic: 13.8 us -> none  [local(): running = running + panel_product(tiles_a, cols_a, count_a, rows_dense)]
  transfers between devices with their start and end apart: 24 -> 0, of which waited for: 10 -> 0; matrix products, arithmetic and copies ran while one was open for 42% -> 0% of each run, Pallas kernels for 0% -> 0%
where the time goes in v2:
time: 39.4 us; the launch traced here: 39.3 us
  Pallas kernels  36.6 us (93%)
  local copies, waits for them, and re-layouts  2.65 us (7%)
    pallas_call x1, Pallas kernels, local_fast(): pl.pallas_call(functools.partial(gather_multiply, n_col), out_shape=jax.S...  36.6 us
    unnamed x1, local copies, waits for them, and re-layouts  2.65 us

profile of v2, /device:TPU:2, one launch (start us, length us, event | category | flops | bytes accessed | tf_op | source)
XLA Modules:
  0.0 39.3 jit_solution(15486463398747699959)
XLA Ops:
  0.0 36.6 %shard_map.64 = bf16[512,1536]{1,0:T(8,128)(2,1)} custom-call(s32[2,8]{1,0:T(2,128)} %bitcast.16, s32[1,8]{1,0:T(1,128)} %bitcast.17, s32[4,1,16]{2,1,0:T(1,128)} %bitcast.14, s32[4,1,16]{2,1,0:T(1,128)} %bitcast.15, bf16[8,2,128,128]{3,2,1,0:T(8,128)(2,1)} %bitcast.13, bf16[4,16,128,128]{3,2,1,0:T(8,128)(2,1)} %bitcast.12), custom_call_target="tpu_custom_call" | custom-call | tf_op jit(solution)/shard_map/pallas_call | solution.py:427
  36.6 2.7 %copy.10 = bf16[512,1536]{1,0:T(8,128)(2,1)} copy(bf16[512,1536]{1,0:T(8,128)(2,1)} %shard_map.64) | data formatting | bytes 3145728

commit v3 on v2

--- a/solution.py
+++ b/solution.py
@@ -140,6 +140,7 @@
 
 REACH = SHIFTS + 1
 CHUNKS = 4
+WIDTH = 1
 MESH_ID = pl.DeviceIdType.MESH
 
 
@@ -157,7 +158,8 @@
     out_cols = out_ref.shape[1] // size
     terms = SHIFTS * 2 * per_row
     zero_at = half * terms
-    units = [(d, r) for d in range(2) for r in range(half)]
+    parts = half // WIDTH
+    units = [(d, pl.ds(h * WIDTH, WIDTH)) for d in range(2) for h in range(parts)]
     count_u = len(units)
     step_b = inner // CHUNKS
 
@@ -222,10 +224,14 @@
             )
 
     swap = [
-        remote(a_ref.at[(1 - dep) * half + r], A.at[0, 1, r], send_a.at[0, r], recv_a.at[0, half + r], twin_dev)
-        for r in range(half)
+        remote(
+            a_ref.at[pl.ds((1 - dep) * half + h * WIDTH, WIDTH)], A.at[0, 1, pl.ds(h * WIDTH, WIDTH)],
+            send_a.at[0, h], recv_a.at[0, parts + h], twin_dev,
+        )
+        for h in range(parts)
     ]
-    first = [a_ref.at[dep * half + r] for r in range(half)] + [A.at[0, 1, r] for r in range(half)]
+    first = [a_ref.at[pl.ds(dep * half + h * WIDTH, WIDTH)] for h in range(parts)]
+    first += [A.at[0, 1, pl.ds(h * WIDTH, WIDTH)] for h in range(parts)]
 
     def to_panel(p, sources, send_row, dev):
         return [
@@ -268,7 +274,7 @@
         copy.start()
     for copy in index_copies[2:-6]:
         copy.start()
-    for r in range(half):
+    for r in range(parts):
         chain[r].start()
         swap[r].start()
 
@@ -281,13 +287,13 @@
     for copy in near_b:
         copy.start()
     run[zero_at] = jnp.zeros(run.shape[1:], jnp.float32)
-    for r in range(half):
+    for r in range(parts):
         swap[r].wait_recv()
-        chain[half + r].start()
+        chain[parts + r].start()
 
         @pl.when(side == 1)
         def _():
-            odd1[half + r].start()
+            odd1[parts + r].start()
 
     groups = [(s, m, k, d, far) for k in range(2) for far, s, m in ((0, s_near[k], m_near[k]), (1, s_far[k], m_mine[k]))
               for d in range(2)]
@@ -331,6 +337,8 @@
 
         lax.fori_loop(0, per_row, one, 0)
 
+    begin = count_u // 4
+    lag = begin + count_u * 3 // 8
     for u in range(count_u):
         chain[u].wait_recv()
         chain2[u].start()
@@ -343,10 +351,10 @@
         def _():
             odd3[u].start()
 
-        if u % 2 == 1 and u // 2 < CHUNKS:
-            far_b[u // 2].wait_recv()
-            pass_b[u // 2].start()
-        if u == 1:
+        for c in range(u * CHUNKS // count_u, (u + 1) * CHUNKS // count_u):
+            far_b[c].wait_recv()
+            pass_b[c].start()
+        if u == begin:
             for copy in index_local:
                 copy.wait()
             for copy in index_copies:
@@ -359,14 +367,16 @@
                 copy.start()
             for copy in scalars:
                 copy.wait()
-        if 2 <= u < 2 + half:
-            tables(u - 2, 0)
+        for r in range(half):
+            if u == begin + r * count_u // (2 * half):
+                tables(r, 0)
 
     def near_unit(u):
         odd3[u].wait_recv()
-        d, r = units[u]
+        d, h = u // parts, u % parts
         for t in range(per_row):
-            product(4 + d, d, r, t, (Bn1, Gn1)[d])
+            for r in range(h * WIDTH, (h + 1) * WIDTH):
+                product(4 + d, d, r, t, (Bn1, Gn1)[d])
 
     done = 0
     for u in range(count_u):
@@ -376,10 +386,10 @@
         def _():
             even3[u].start()
 
-        if u % 2 == 1 and u // 2 < CHUNKS:
-            far_b[CHUNKS + u // 2].wait_recv()
-            pass_b[CHUNKS + u // 2].start()
-        if u == 2:
+        for c in range(CHUNKS + u * CHUNKS // count_u, CHUNKS + (u + 1) * CHUNKS // count_u):
+            far_b[c].wait_recv()
+            pass_b[c].start()
+        if u == begin:
             a_local.wait()
             for copy in b_local:
                 copy.wait()
@@ -389,9 +399,10 @@
                 copy.wait_recv()
             for c in range(CHUNKS):
                 pass_b[c].wait_recv()
-        if 2 <= u < 6:
-            whole_group(u - 2, (Bn0, Gn0, Bf0, Gf0)[u - 2])
-        if u >= 5:
+        for g, right in enumerate((Bn0, Gn0, Bf0, Gf0)):
+            if u == begin + g * count_u // 8:
+                whole_group(g, right)
+        if u >= lag:
             near_unit(done)
             done += 1
     for u in range(done, count_u):
@@ -424,7 +435,7 @@
     vmem = pl.BlockSpec(memory_space=pltpu.VMEM)
     index_shapes = [(panels, per_row, block_rows), (panels, 1, block_rows), (4, slots, 1, inner), (4, slots, 1, inner)]
     right = pltpu.VMEM((inner, size, size), jnp.bfloat16)
-    return pl.pallas_call(
+    call = pl.pallas_call(
         functools.partial(gather_multiply, n_col),
         out_shape=jax.ShapeDtypeStruct((half * size, BC * size), jnp.bfloat16),
         in_specs=[hbm] * 6,
@@ -447,16 +458,18 @@
             pltpu.SemaphoreType.DMA((7,)),
         ],
         compiler_params=pltpu.CompilerParams(
-            collective_id=0, has_side_effects=True, vmem_limit_bytes=65200000
+            collective_id=0, has_side_effects=True, vmem_limit_bytes=40 * 1024 * 1024
         ),
-    )(
+    )
+    operands = [
         jnp.swapaxes(a_cols.reshape(block_rows, per_row), 0, 1),
         a_count.reshape(1, block_rows),
         b_cols.reshape(slots, 1, inner),
         b_count.reshape(slots, 1, inner),
         a_tiles.reshape(block_rows, per_row, size, size),
         b_tiles.reshape(slots, inner, size, size),
-    )
+    ]
+    return call(*(pltpu.with_memory_space_constraint(x, pltpu.HBM) for x in operands))
 
 
 def solution(mesh):

time: 39.4 us -> 36.7 us (0.931)
  local copies, waits for them, and re-layouts: 2.65 us -> 1.15 us
  Pallas kernels: 36.6 us -> 35.4 us
    unnamed x1, local copies, waits for them, and re-layouts: 2.65 us -> 1.15 us
    pallas_call x1, Pallas kernels: 36.6 us -> 35.4 us  [local_fast(): call(*(pltpu.with_memory_space_constraint(x, pltpu.HBM) for x in operands))]
where the time goes in v3:
time: 36.7 us; the launch traced here: 36.5 us
  Pallas kernels  35.4 us (96%)
  local copies, waits for them, and re-layouts  1.15 us (3%)
    pallas_call x1, Pallas kernels, local_fast(): call(*(pltpu.with_memory_space_constraint(x, pltpu.HBM) for x in operands))  35.4 us
    unnamed x1, local copies, waits for them, and re-layouts  1.15 us

profile of v3, /device:TPU:2, one launch (start us, length us, event | category | flops | bytes accessed | tf_op | source)
XLA Modules:
  0.0 36.5 jit_solution(6725883281973962387)
XLA Ops:
  0.0 35.4 %shard_map.64 = bf16[512,1536]{1,0:T(8,128)(2,1)S(1)} custom-call(s32[2,8]{1,0:T(2,128)} %bitcast.16, s32[1,8]{1,0:T(1,128)} %bitcast.17, s32[4,1,16]{2,1,0:T(1,128)} %bitcast.14, s32[4,1,16]{2,1,0:T(1,128)} %bitcast.15, bf16[8,2,128,128]{3,2,1,0:T(8,128)(2,1)} %bitcast.13, bf16[4,16,128,128]{3,2,1,0:T(8,128)(2,1)} %bitcast.12), custom_call_target="tpu_custom_call" | custom-call | tf_op jit(solution)/shard_map/pallas_call | solution.py:472
  35.4 1.1 %copy.10 = bf16[512,1536]{1,0:T(8,128)(2,1)} copy(bf16[512,1536]{1,0:T(8,128)(2,1)S(1)} %shard_map.64) | data formatting | bytes 3145728
